TPU v7x, 32 devices: a whole 2x2x4 slice. The times are simulated.
32 devices in a mesh: lon: 8 (over z, core), mem: 4 (over y, x).
Axes of the slice: x: 2, y: 2, z: 4, core: 2. Of those that a mesh axis runs over, the one named last changes fastest.
Arguments:
- members: float32 [32, 4, 192, 256], P('mem', None, 'lon'), may hold values from -6 to 6
- courant_lon: float32 [4, 192, 256], P(None, 'lon'), may hold values from -0.55 to 0.55
- courant_lat: float32 [4, 192, 256], P(None, 'lon'), may hold values from -0.4 to 0.4
- vert_modes: float32 [2, 4], replicated, may hold values from -1 to 1
- horiz_modes: float32 [4, 192, 256], P(None, 'lon'), may hold values from -1 to 1
- obs_index: int32 [16384], P('lon'), may hold values from 0 to 24575
- obs_count: int32 [8], P('lon'), may hold values from 1024 to 2048, as said below
- obs_value: float32 [16384], P('lon'), may hold values from -6 to 6
- obs_var: float32 [16384], P('lon'), may hold values from 2 to 48
Outputs:
- prior_trajectories: float32 [32, 4, 192, 256], P('mem', None, 'lon')
- analysis_mean: float32 [4, 192, 256], P(None, 'lon')
Inputs may be any that keep to these rules, and one draw needn't show every extreme that they name: `obs_index`: index of a cell within the band's own block: level, then longitude within the band, then latitude. Each band uses its first obs_count slots; some band uses all 2048.
All inputs are finite; a program needn't handle non-finite values.
Results may differ from a plain program's by a relative error of at most 0.0001.
Values sent between devices are 32-bit elements; how exact they have to be, the bound alone decides.
A program may use at most 128 MiB of HBM per device.

v0:
```python
import jax
import jax.numpy as jnp
from jax import lax
from jax.sharding import PartitionSpec as P

KV = 2
KH = 4
ADV_STEPS = 2


def padded(block, sides, width):
    for axis, dim in sides:
        count = lax.axis_size(axis)
        forward = [(i, i + 1) for i in range(count - 1)]
        forward.append((count - 1, 0))
        backward = [(target, source) for source, target in forward]
        low = lax.ppermute(
            lax.slice_in_dim(block, block.shape[dim] - width, None, axis=dim), axis, forward
        )
        high = lax.ppermute(lax.slice_in_dim(block, 0, width, axis=dim), axis, backward)
        block = jnp.concatenate([low, block, high], axis=dim)
    return block


def update(centre, western, eastern, flow_lon, flow_lat):
    zero_col = jnp.zeros_like(centre[..., :1])
    south_boundary = jnp.concatenate([zero_col, centre[..., :-1]], axis=-1)
    northern = jnp.concatenate([centre[..., 1:], zero_col], axis=-1)
    result = centre - jnp.maximum(flow_lon, 0.0) * (centre - western)
    result = result - jnp.minimum(flow_lon, 0.0) * (eastern - centre)
    result = result - jnp.maximum(flow_lat, 0.0) * (centre - south_boundary)
    result = result - jnp.minimum(flow_lat, 0.0) * (northern - centre)
    return result


def per_device(
    members,
    courant_lon,
    courant_lat,
    vert_modes,
    horiz_modes,
    obs_index,
    obs_count,
    obs_value,
    obs_var,
):
    mem_dev, layer_tally, band_width, lat_rows = members.shape
    sample_tally_overall = mem_dev * lax.axis_size("mem")
    rim_depth = ADV_STEPS
    stacked = jnp.concatenate(
        [members.reshape(mem_dev * layer_tally, band_width, lat_rows), courant_lon, courant_lat],
        axis=0,
    )
    extended = padded(stacked, (("lon", 1),), rim_depth)
    split_at = mem_dev * layer_tally
    prognostic_vector = extended[:split_at].reshape(
        mem_dev, layer_tally, band_width + 2 * rim_depth, lat_rows
    )
    flow_lon_ext = extended[split_at : split_at + layer_tally]
    meridional_wind_padded = extended[split_at + layer_tally :]
    for section in range(rim_depth):
        out_cols = band_width + 2 * (rim_depth - 1 - section)
        first_col = section + 1
        prognostic_vector = update(
            prognostic_vector[:, :, 1 : out_cols + 1],
            prognostic_vector[:, :, 0:out_cols],
            prognostic_vector[:, :, 2 : out_cols + 2],
            flow_lon_ext[:, first_col : first_col + out_cols],
            meridional_wind_padded[:, first_col : first_col + out_cols],
        )
    sample_centroid = lax.psum(jnp.sum(prognostic_vector, axis=0), "mem") / sample_tally_overall
    sample_departure = prognostic_vector - sample_centroid[None]
    norm_scale = (sample_tally_overall - 1) ** (-0.5)
    obs_slots = obs_index.shape[0]
    band_cells = band_width * lat_rows
    level_idx = obs_index // band_cells
    within = obs_index % band_cells
    anomaly_obs = jnp.take(sample_departure.reshape(mem_dev, -1), obs_index, axis=1)
    mean_obs = jnp.take(sample_centroid.reshape(-1), obs_index)
    vert_obs = jnp.take(vert_modes, level_idx, axis=1)
    horiz_obs = jnp.take(horiz_modes.reshape(KH, -1), within, axis=1)
    modes_obs = (vert_obs[:, None, :] * horiz_obs[None, :, :]).reshape(KV * KH, obs_slots)
    live_mask = (jnp.arange(obs_slots, dtype=jnp.int32) < obs_count[0]).astype(jnp.float32)
    obs_perts = (
        anomaly_obs[:, None, :] * modes_obs[None, :, :] * (live_mask * norm_scale)[None, None, :]
    )
    obs_perts = obs_perts.reshape(mem_dev * KV * KH, obs_slots)
    inv_var = live_mask / obs_var
    innovation = obs_value - mean_obs
    all_perts = lax.all_gather(obs_perts, "mem", axis=0, tiled=True)
    gram_part = jnp.dot(all_perts * inv_var[None, :], all_perts.T, precision=lax.Precision.HIGHEST)
    side_part = jnp.dot(all_perts, inv_var * innovation, precision=lax.Precision.HIGHEST)
    gram_matrix, right_side = lax.psum((gram_part, side_part), "lon")
    system = jnp.eye(gram_matrix.shape[0], dtype=jnp.float32) + gram_matrix
    factor = jnp.linalg.cholesky(system)
    weights = jax.scipy.linalg.cho_solve((factor, True), right_side)
    w_mat = weights.reshape(sample_tally_overall, KV * KH)
    w_local = lax.dynamic_slice_in_dim(w_mat, lax.axis_index("mem") * mem_dev, mem_dev, 0)
    mode_coef = jnp.einsum(
        "mk,mlij->klij", w_local, sample_departure, precision=lax.Precision.HIGHEST
    )
    mode_coef = mode_coef.reshape(KV, KH, layer_tally, band_width, lat_rows)
    inc_part = (
        jnp.einsum(
            "al,bij,ablij->lij", vert_modes, horiz_modes, mode_coef, precision=lax.Precision.HIGHEST
        )
        * norm_scale
    )
    posterior_adjustment = lax.psum(inc_part, "mem")
    return (prognostic_vector, sample_centroid + posterior_adjustment)


def solution(mesh):
    placed = (
        P("mem", None, "lon", None),
        P(None, "lon", None),
        P(None, "lon", None),
        P(),
        P(None, "lon", None),
        P("lon"),
        P("lon"),
        P("lon"),
        P("lon"),
    )
    return jax.shard_map(
        per_device,
        mesh=mesh,
        in_specs=placed,
        out_specs=(P("mem", None, "lon", None), P(None, "lon", None)),
        check_vma=False,
    )
```

profile of v0, /device:TPU:0, one launch (start us, length us, event | category | flops | bytes accessed | tf_op | source)
XLA Modules:
  0.0 332.7 jit_solution(16638624239704680310)
XLA Ops:
  7.2 1.2 pad_maximum_fusion.5
  8.4 0.5 collective-permute-start
  8.9 4.1 %collective-permute-start.1 = (f32[40,2,256]{2,1,0:T(2,128)S(1)}, f32[40,2,256]{2,1,0:T(2,128)S(1)}, u32[]{:S(2)}, u32[]{:S(2)}) collective-permute-start(f32[40,2,256]{2,1,0:T(2,128)S(1)} %get-tuple-element.36), channel_id=1, source_target_pairs={{4,0},{8,4},{12,8},{16,12},{20,16},{24,20},{28,24},{0,28},{5,1},{9... | collective-permute-start | bytes 245768 | tf_op jit(solution)/shard_map/ppermute | solution.py:20
  13.0 0.7 compare_and_fusion.1
  13.8 0.7 fusion.30
  14.5 0.8 copy.32
  15.2 5.5 %gather_fusion.1 = f32[2048,2]{1,0:T(8,128)S(1)} fusion(f32[2,4]{0,1:T(4,128)S(1)} %copy.32, s32[2048]{0:T(1024)S(1)} %get-tuple-element.46), kind=kCustom, calls=%fused_computation.1 | custom fusion | bytes 40960 | tf_op jit(solution)/shard_map/jit(_take)/gather | solution.py:80
  20.7 0.3 select_bitcast_fusion.1
  21.0 0.3 copy.33
  21.4 2.3 copy.34
  23.6 7.4 %gather_fusion.2 = f32[2048,4]{1,0:T(8,128)S(1)} fusion(f32[4,6144]{0,1:T(8,128)} %bitcast.119, s32[2048]{0:T(1024)S(1)} %get-tuple-element.47), kind=kCustom, calls=%fused_computation.2 | custom fusion | bytes 73728 | tf_op jit(solution)/shard_map/jit(_take)/gather | solution.py:81
  31.1 0.3 select_bitcast_fusion
  31.4 0.3 copy.35
  32.6 0.2 pad_maximum_fusion
  32.8 0.1 slice.157
  32.9 0.4 fusion.43
  33.4 0.7 fusion.9
  34.1 0.3 fusion.42
  34.4 1.2 fusion.39
  35.6 41.8 %all-reduce.9.cloned.1.call-done = f32[4,24,256]{2,1,0:T(8,128)} async-done(((f32[4,24,256]{2,1,0:T(8,128)}), f32[4,24,256]{2,1,0:T(8,128)}) %all-reduce.9.cloned.1.call-update) | async-done | bytes 98320 | tf_op jit(solution)/shard_map/psum | solution.py:71
  77.5 0.9 broadcast_multiply_fusion
  78.5 6.6 %copy.30 = f32[8,4,24,256]{0,3,2,1:T(8,128)} copy(f32[8,4,24,256]{3,2,1,0:T(8,128)S(1)} %broadcast_subtract_fusion) | data formatting | bytes 1572864 | tf_op jit(solution)/shard_map/sub | solution.py:72
  85.1 11.8 %gather_fusion.3 = f32[2048]{0:T(1024)S(1)} fusion(f32[24576]{0:T(1024)S(1)} %bitcast.112, s32[2048]{0:T(1024)S(1)} %get-tuple-element.45), kind=kCustom, calls=%fused_computation.3 | custom fusion | bytes 24576 | tf_op jit(solution)/shard_map/jit(_take)/gather | solution.py:79
  96.9 10.0 %gather_fusion = f32[2048,8]{1,0:T(8,128)S(1)} fusion(f32[8,24576]{0,1:T(8,128)} %bitcast.113, s32[2048]{0:T(1024)S(1)} %get-tuple-element.45), kind=kCustom, calls=%fused_computation | custom fusion | bytes 139264 | tf_op jit(solution)/shard_map/jit(_take)/gather | solution.py:78
  107.0 0.3 select_bitcast_fusion.2
  107.4 0.3 copy.31
  107.6 0.9 bitcast_multiply_fusion
  108.6 0.1 copy.51
  108.8 35.2 %all-gather.2.cloned.1.call-done = f32[256,2048]{1,0:T(8,128)} async-done(((f32[64,2048]{1,0:T(8,128)}), f32[256,2048]{1,0:T(8,128)}) %all-gather.2.cloned.1.call-update) | async-done | bytes 2097168 | tf_op jit(solution)/shard_map/all_gather | solution.py:90
  144.0 5.0 %fusion = f32[256,256]{0,1:T(8,128)} fusion(f32[256,2048]{1,0:T(8,128)} %all-gather.2.cloned.1.call-done, f32[2048]{0:T(1024)S(1)} %get-tuple-element.19), kind=kOutput, calls=%fused_computation.6 | convolution fusion | flops 1611137024 | bytes 2367488 | tf_op jit(solution)/shard_map/dot_general | solution.py:91
  149.1 1.7 fusion.44
  150.8 16.6 %psum.30 = f32[256]{0:T(256)S(1)} all-reduce(f32[256]{0:T(256)S(1)} %bitcast.124), channel_id=1, replica_groups=mesh['lon'=8,'mem'=4] {'lon'}, use_global_device_ids=true, to_apply=%region_7.8 | all-reduce | flops 256 | bytes 2048 | tf_op jit(solution)/shard_map/psum | solution.py:93
  167.4 36.7 %all-reduce.11.cloned.1.call-done = f32[256,256]{0,1:T(8,128)} async-done(((f32[256,256]{0,1:T(8,128)}), f32[256,256]{0,1:T(8,128)}) %all-reduce.11.cloned.1.call-update) | async-done | bytes 262160 | tf_op jit(solution)/shard_map/psum | solution.py:93
  204.1 1.0 convert_add_fusion
  205.1 0.1 copy.37
  205.2 1.0 fusion.19
  206.2 11.7 %cholesky.50 = f32[128,128]{1,0:T(8,128)S(1)} custom-call(f32[128,128]{1,0:T(8,128)S(1)} %cholesky.118), custom_call_target="Cholesky" | custom-call | tf_op jit(solution)/shard_map/jit(cholesky)/cholesky | solution.py:95
  218.0 0.7 compare_reduce_fusion.1
  218.7 9.8 %custom-call.18 = f32[1,128,128]{1,2,0:T(8,128)S(1)} custom-call(f32[1,128,128]{2,1,0:T(8,128)S(1)} %get-tuple-element.44), custom_call_target="InvertDiagBlocksLowerTriangular" | custom-call | tf_op jit(solution)/shard_map/jit(cholesky)/cholesky | solution.py:95
  228.5 0.2 constant_dynamic-update-slice_fusion.1
  228.7 0.3 convolution_subtract_fusion
  229.0 11.7 %cholesky.105 = f32[128,128]{1,0:T(8,128)S(1)} custom-call(f32[128,128]{1,0:T(8,128)S(1)} %convolution_subtract_fusion), custom_call_target="Cholesky" | custom-call | tf_op jit(solution)/shard_map/jit(cholesky)/cholesky | solution.py:95
  240.7 0.6 compare_reduce_fusion
  242.6 0.1 triangular_solve.73
  242.6 3.8 %while.1 = (s32[]{:T(128)}, f32[256,256]{1,0:T(8,128)S(1)}, s32[2,2]{1,0:T(2,128)S(1)}, f32[2,128,128]{2,1,0:T(8,128)S(1)}, s32[]{:T(128)}) while((s32[]{:T(128)}, f32[256,256]{1,0:T(8,128)S(1)}, s32[2,2]{1,0:T(2,128)S(1)}, f32[2,128,128]{2,1,0:T(8,128)S(1)}, s32[]{:T(128)}) %tuple.44), condition=%wide.while_cond, body=%wide.while_body.sunk | while | flops 2 | bytes 131189 | solution.py:96
  242.6 0.6 fusion.57
  243.2 1.3 bitcast_dynamic-update-slice_fusion.2
  244.5 0.6 fusion.57
  245.2 1.3 bitcast_dynamic-update-slice_fusion.2
  246.4 19.9 %custom-call.19 = f32[2,128,128]{1,2,0:T(8,128)S(1)} custom-call(f32[2,128,128]{2,1,0:T(8,128)S(1)} %get-tuple-element.9), custom_call_target="InvertDiagBlocksLowerTriangular" | custom-call | tf_op jit(solution)/shard_map/jit(_cho_solve)/triangular_solve | solution.py:96
  266.3 0.2 fusion.25
  266.5 0.2 fusion.5
  266.7 0.2 convolution_bitcast_fusion.3
  266.9 0.2 convolution_bitcast_fusion.2
  267.1 0.2 fusion.3
  267.3 0.2 convolution_bitcast_fusion
  267.5 0.1 reshape.169
  267.6 13.6 %fusion.31 = f32[8,4,24,256]{3,0,2,1:T(8,128)S(1)} fusion(f32[8,4,24,256]{0,3,2,1:T(8,128)} %copy.30, f32[32,8]{1,0:T(8,128)S(1)} %reshape.169, s32[]{:T(128)S(6)} %select_n.71), kind=kOutput, calls=%fused_computation.98 | convolution fusion | flops 18874368 | bytes 1576964 | tf_op jit(solution)/shard_map/mk,mlij->klij/dot_general | solution.py:99
  281.2 0.2 reshape.170
  281.5 0.6 multiply_reduce_fusion
  282.1 0.8 fusion.20
  283.0 0.7 bitcast_multiply_fusion.1
  283.6 41.0 %all-reduce.13.cloned.1.call-done = f32[4,24,256]{2,1,0:T(8,128)} async-done(((f32[4,24,256]{2,1,0:T(8,128)}), f32[4,24,256]{2,1,0:T(8,128)}) %all-reduce.13.cloned.1.call-update) | async-done | bytes 98320 | tf_op jit(solution)/shard_map/psum | solution.py:109
  324.6 1.5 fusion.38
  (53 shorter events, 0.8 us)
Async XLA Ops:
  7.2 70.3 %all-reduce.9.cloned.1.call-start = ((), (), s32[]{:S(2)}) async-start(), calls=%async_computation | async-start | bytes 196608 | tf_op jit(solution)/shard_map/psum | solution.py:71
  7.2 14.2 %copy-start.5 = (f32[4,24,256]{2,1,0:T(8,128)S(1)}, f32[4,24,256]{2,1,0:T(8,128)}, u32[]{:S(2)}) copy-start(f32[4,24,256]{2,1,0:T(8,128)} %param.13) | copy-start | bytes 294916
  8.4 24.1 %collective-permute-start = (f32[40,2,256]{2,1,0:T(2,128)S(1)}, f32[40,2,256]{2,1,0:T(2,128)S(1)}, u32[]{:S(2)}, u32[]{:S(2)}) collective-permute-start(f32[40,2,256]{2,1,0:T(2,128)S(1)} %get-tuple-element.35), channel_id=1, source_target_pairs={{0,4},{4,8},{8,12},{12,16},{16,20},{20,24},{24,28},{28,0},{1,5},{5... | collective-permute-start | bytes 245768 | tf_op jit(solution)/shard_map/ppermute | solution.py:17
  8.9 23.6 %collective-permute-start.1 = (f32[40,2,256]{2,1,0:T(2,128)S(1)}, f32[40,2,256]{2,1,0:T(2,128)S(1)}, u32[]{:S(2)}, u32[]{:S(2)}) collective-permute-start(f32[40,2,256]{2,1,0:T(2,128)S(1)} %get-tuple-element.36), channel_id=1, source_target_pairs={{4,0},{8,4},{12,8},{16,12},{20,16},{24,20},{28,24},{0,28},{5,1},{9... | collective-permute-start | bytes 245768 | tf_op jit(solution)/shard_map/ppermute | solution.py:20
  23.6 8.2 %copy-start.3 = (f32[4,24,256]{2,1,0:T(8,128)S(1)}, f32[4,24,256]{2,1,0:T(8,128)}, u32[]{:S(2)}) copy-start(f32[4,24,256]{2,1,0:T(8,128)} %param.11) | copy-start | bytes 294916
  23.6 8.2 %copy-start.4 = (f32[4,24,256]{2,1,0:T(8,128)S(1)}, f32[4,24,256]{2,1,0:T(8,128)}, u32[]{:S(2)}) copy-start(f32[4,24,256]{2,1,0:T(8,128)} %param.10) | copy-start | bytes 294916
  23.6 8.9 %copy-start.1 = (f32[8,4,24,256]{3,2,1,0:T(8,128)S(1)}, f32[8,4,24,256]{3,2,1,0:T(8,128)}, u32[]{:S(2)}) copy-start(f32[8,4,24,256]{3,2,1,0:T(8,128)} %param.9) | copy-start | bytes 2359300
  35.6 49.5 %copy-start.2 = (f32[8,4,24,256]{3,2,1,0:T(8,128)}, f32[8,4,24,256]{3,2,1,0:T(8,128)S(1)}, u32[]{:S(2)}) copy-start(f32[8,4,24,256]{3,2,1,0:T(8,128)S(1)} %get-tuple-element.22) | copy-start | bytes 2359300
  35.6 108.4 %all-gather.2.cloned.1.call-start = ((), (), s32[]{:S(2)}) async-start(), calls=%async_computation.1 | async-start | bytes 2621440 | tf_op jit(solution)/shard_map/all_gather | solution.py:90
  85.1 21.9 %copy-start.7 = (s32[2048]{0:T(1024)S(1)}, s32[2048]{0:T(1024)}, u32[]{:S(2)}) copy-start(s32[2048]{0:T(1024)} %param.14) | copy-start | bytes 24580
  85.1 21.9 %copy-start.8 = (f32[2048]{0:T(1024)S(1)}, f32[2048]{0:T(1024)}, u32[]{:S(2)}) copy-start(f32[2048]{0:T(1024)} %param.16) | copy-start | bytes 24580
  85.1 21.9 %copy-start.9 = (f32[2048]{0:T(1024)S(1)}, f32[2048]{0:T(1024)}, u32[]{:S(2)}) copy-start(f32[2048]{0:T(1024)} %param.17) | copy-start | bytes 24580
  107.0 1.6 copy-start.10
  108.5 95.6 %all-reduce.11.cloned.1.call-start = ((), (), s32[]{:S(2)}) async-start(), calls=%async_computation.2 | async-start | bytes 524288 | tf_op jit(solution)/shard_map/psum | solution.py:93
  144.0 5.1 %copy-start = (f32[256,2048]{1,0:T(8,128)S(1)}, f32[256,2048]{1,0:T(8,128)}, u32[]{:S(2)}) copy-start(f32[256,2048]{1,0:T(8,128)} %all-gather.2.cloned.1.call-done) | copy-start | bytes 6291460
  149.0 175.6 %all-reduce.13.cloned.1.call-start = ((), (), s32[]{:S(2)}) async-start(), calls=%async_computation.3 | async-start | bytes 196608 | tf_op jit(solution)/shard_map/psum | solution.py:109
  281.2 43.4 %copy-start.6 = (f32[4,24,256]{2,1,0:T(8,128)S(1)}, f32[4,24,256]{2,1,0:T(8,128)}, u32[]{:S(2)}) copy-start(f32[4,24,256]{2,1,0:T(8,128)} %all-reduce.9.cloned.1.call-done) | copy-start | bytes 294916
Sparse Core Ops, SparseCore 0:
  35.7 41.7 all-reduce.8
  108.7 35.2 all-gather.1
  149.1 54.9 all-reduce.10
  283.8 40.8 all-reduce.12
where the time goes:
time: 333 us
  waiting for transfers between devices  155 us (47%)
  other arithmetic  67 us (20%)
  local copies, waits for them, and re-layouts  50.6 us (15%)
  matrix products  22.8 us (7%)
  blocking collectives  16.6 us (5%)
  between operations  16 us (5%)
  starting transfers between devices  4.77 us (1%)
    psum x1, waiting for transfers between devices, per_device(): lax.psum(jnp.sum(prognostic_vector, axis=0), 'mem') / sample_tally_overall  41.8 us
    psum x1, waiting for transfers between devices, per_device(): posterior_adjustment = lax.psum(inc_part, 'mem')  41 us
    psum x1, waiting for transfers between devices, per_device(): gram_matrix, right_side = lax.psum((gram_part, side_part), 'lon')  36.7 us
    all_gather x1, waiting for transfers between devices, per_device(): all_perts = lax.all_gather(obs_perts, 'mem', axis=0, tiled=True)  35.2 us
    another operation x7, other arithmetic, per_device(): factor = jnp.linalg.cholesky(system)  34.6 us
    another operation x4, other arithmetic, per_device(): weights = jax.scipy.linalg.cho_solve((factor, True), right_side)  20 us
    psum x1, blocking collectives, per_device(): gram_matrix, right_side = lax.psum((gram_part, side_part), 'lon')  16.6 us
    dot_general x1, matrix products, per_device(): jnp.einsum('mk,mlij->klij', w_local, sample_departure, precision=lax.Prec...  13.6 us
  transfers between devices with their start and end apart: 6, of which 4 were waited for; matrix products, arithmetic and copies ran while one was open for 6% of the time, Pallas kernels for 0%

commit v1 on v0

--- a/solution.py
+++ b/solution.py
@@ -1,3 +1,4 @@
+import functools
 import jax
 import jax.numpy as jnp
 from jax import lax
@@ -6,6 +7,14 @@
 KV = 2
 KH = 4
 ADV_STEPS = 2
+
+
+def _time_regions(page, dev_axis):
+    arr_out = jnp.sum(lax.all_gather(page, dev_axis), axis=0)
+    return arr_out
+
+
+_expand_core = functools.partial(_time_regions, dev_axis="mem")
 
 
 def padded(block, sides, width):
@@ -68,7 +77,7 @@
             flow_lon_ext[:, first_col : first_col + out_cols],
             meridional_wind_padded[:, first_col : first_col + out_cols],
         )
-    sample_centroid = lax.psum(jnp.sum(prognostic_vector, axis=0), "mem") / sample_tally_overall
+    sample_centroid = _expand_core(jnp.sum(prognostic_vector, axis=0)) / sample_tally_overall
     sample_departure = prognostic_vector - sample_centroid[None]
     norm_scale = (sample_tally_overall - 1) ** (-0.5)
     obs_slots = obs_index.shape[0]

time: 333 us -> 306 us (0.919)
  waiting for transfers between devices: 155 us -> 111 us
  blocking collectives: 16.6 us -> 27.1 us
  other arithmetic: 67 us -> 72 us
    psum x1 -> x0, waiting for transfers between devices: 41.8 us -> none  [per_device(): lax.psum(jnp.sum(prognostic_vector, axis=0), 'mem') / sample_tally_overall]
    all_gather x0 -> x1, blocking collectives: none -> 10.5 us  [_time_regions(): arr_out = jnp.sum(lax.all_gather(page, dev_axis), axis=0)]
  transfers between devices with their start and end apart: 6 -> 5, of which waited for: 4 -> 3; matrix products, arithmetic and copies ran while one was open for 6% -> 8% of each run, Pallas kernels for 0% -> 0%
where the time goes in v1:
time: 306 us
  waiting for transfers between devices  111 us (36%)
  other arithmetic  72 us (24%)
  local copies, waits for them, and re-layouts  51.7 us (17%)
  blocking collectives  27.1 us (9%)
  matrix products  22.8 us (7%)
  between operations  16 us (5%)
  starting transfers between devices  4.67 us (2%)
    psum x1, waiting for transfers between devices, per_device(): posterior_adjustment = lax.psum(inc_part, 'mem')  41 us
    psum x1, waiting for transfers between devices, per_device(): gram_matrix, right_side = lax.psum((gram_part, side_part), 'lon')  36.7 us
    another operation x7, other arithmetic, per_device(): factor = jnp.linalg.cholesky(system)  34.6 us
    all_gather x1, waiting for transfers between devices, per_device(): all_perts = lax.all_gather(obs_perts, 'mem', axis=0, tiled=True)  33.7 us
    another operation x4, other arithmetic, per_device(): weights = jax.scipy.linalg.cho_solve((factor, True), right_side)  20 us
    psum x1, blocking collectives, per_device(): gram_matrix, right_side = lax.psum((gram_part, side_part), 'lon')  16.6 us
    dot_general x1, matrix products, per_device(): jnp.einsum('mk,mlij->klij', w_local, sample_departure, precision=lax.Prec...  13.6 us
    gather x1, local copies, waits for them, and re-layouts, per_device(): mean_obs = jnp.take(sample_centroid.reshape(-1), obs_index)  11.8 us
  transfers between devices with their start and end apart: 5, of which 3 were waited for; matrix products, arithmetic and copies ran while one was open for 8% of the time, Pallas kernels for 0%

profile of v1, /device:TPU:0, one launch (start us, length us, event | category | flops | bytes accessed | tf_op | source)
XLA Modules:
  0.0 305.8 jit_solution(1794007520540053138)
XLA Ops:
  7.2 1.8 pad_maximum_fusion.5
  9.0 0.5 collective-permute-start
  9.5 4.1 %collective-permute-start.1 = (f32[40,2,256]{2,1,0:T(2,128)}, f32[40,2,256]{2,1,0:T(2,128)}, u32[]{:S(2)}, u32[]{:S(2)}) collective-permute-start(f32[40,2,256]{2,1,0:T(2,128)} %get-tuple-element.36), channel_id=1, source_target_pairs={{4,0},{8,4},{12,8},{16,12},{20,16},{24,20},{28,24},{0,28},{5,1},{9... | collective-permute-start | bytes 245768 | tf_op jit(solution)/shard_map/ppermute | solution.py:29
  13.6 1.3 compare_and_fusion.1
  14.9 1.3 fusion.30
  16.2 1.6 broadcast_maximum_fusion.2
  18.5 0.8 copy.42
  19.2 5.5 %gather_fusion.1 = f32[2048,2]{1,0:T(8,128)S(1)} fusion(f32[2,4]{0,1:T(4,128)S(1)} %copy.42, s32[2048]{0:T(1024)S(1)} %get-tuple-element.46), kind=kCustom, calls=%fused_computation.1 | custom fusion | bytes 40960 | tf_op jit(solution)/shard_map/jit(_take)/gather | solution.py:89
  24.7 0.3 select_bitcast_fusion.1
  25.0 0.9 copy.43
  26.0 2.2 copy.44
  28.1 7.4 %gather_fusion.2 = f32[2048,4]{1,0:T(8,128)S(1)} fusion(f32[4,6144]{0,1:T(8,128)} %bitcast.120, s32[2048]{0:T(1024)S(1)} %get-tuple-element.47), kind=kCustom, calls=%fused_computation.2 | custom fusion | bytes 73728 | tf_op jit(solution)/shard_map/jit(_take)/gather | solution.py:90
  35.6 1.0 select_bitcast_fusion
  36.6 0.3 copy.45
  36.9 0.7 broadcast_multiply_fusion.1
  37.8 1.1 pad_maximum_fusion
  38.9 0.4 fusion.43
  39.4 0.8 broadcast_maximum_fusion.1
  40.2 0.7 fusion.9
  40.9 0.3 fusion.42
  41.2 0.6 copy-done.6
  41.8 0.5 fusion.39
  42.3 10.5 %all-gather = f32[16,24,256]{2,1,0:T(8,128)S(1)} all-gather(f32[4,24,256]{2,1,0:T(8,128)S(1)} %get-tuple-element.21), channel_id=2, replica_groups=mesh['lon'=8,'mem'=4] {'mem'}, dimensions={0}, use_global_device_ids=true | all-gather | bytes 491520 | tf_op jit(solution)/shard_map/all_gather | solution.py:13
  53.0 6.6 %copy.40 = f32[8,4,24,256]{0,3,2,1:T(8,128)} copy(f32[8,4,24,256]{3,2,1,0:T(8,128)S(1)} %broadcast_subtract_fusion) | data formatting | bytes 1572864 | tf_op jit(solution)/shard_map/sub | solution.py:81
  59.6 11.8 %gather_fusion.3 = f32[2048]{0:T(1024)S(1)} fusion(f32[24576]{0:T(1024)S(1)} %bitcast.113, s32[2048]{0:T(1024)S(1)} %copy-done.8), kind=kCustom, calls=%fused_computation.3 | custom fusion | bytes 24576 | tf_op jit(solution)/shard_map/jit(_take)/gather | solution.py:88
  71.4 10.0 %gather_fusion = f32[2048,8]{1,0:T(8,128)S(1)} fusion(f32[8,24576]{0,1:T(8,128)} %bitcast.114, s32[2048]{0:T(1024)S(1)} %copy-done.8), kind=kCustom, calls=%fused_computation | custom fusion | bytes 139264 | tf_op jit(solution)/shard_map/jit(_take)/gather | solution.py:87
  81.5 0.3 select_bitcast_fusion.2
  81.8 0.3 copy.41
  82.1 0.9 bitcast_multiply_fusion
  83.1 0.1 copy.61
  83.3 33.7 %all-gather.3.cloned.1.call-done = f32[256,2048]{1,0:T(8,128)} async-done(((f32[64,2048]{1,0:T(8,128)}), f32[256,2048]{1,0:T(8,128)}) %all-gather.3.cloned.1.call-update) | async-done | bytes 2097168 | tf_op jit(solution)/shard_map/all_gather | solution.py:99
  116.9 5.0 %fusion = f32[256,256]{0,1:T(8,128)} fusion(f32[256,2048]{1,0:T(8,128)} %all-gather.3.cloned.1.call-done, f32[2048]{0:T(1024)S(1)} %get-tuple-element.19), kind=kOutput, calls=%fused_computation.6 | convolution fusion | flops 1611137024 | bytes 2367488 | tf_op jit(solution)/shard_map/dot_general | solution.py:100
  122.0 1.7 fusion.44
  123.7 16.6 %psum.22 = f32[256]{0:T(256)S(1)} all-reduce(f32[256]{0:T(256)S(1)} %bitcast.126), channel_id=1, replica_groups=mesh['lon'=8,'mem'=4] {'lon'}, use_global_device_ids=true, to_apply=%region_7.8 | all-reduce | flops 256 | bytes 2048 | tf_op jit(solution)/shard_map/psum | solution.py:102
  140.3 36.7 %all-reduce.8.cloned.1.call-done = f32[256,256]{0,1:T(8,128)} async-done(((f32[256,256]{0,1:T(8,128)}), f32[256,256]{0,1:T(8,128)}) %all-reduce.8.cloned.1.call-update) | async-done | bytes 262160 | tf_op jit(solution)/shard_map/psum | solution.py:102
  177.0 1.0 convert_add_fusion
  178.0 0.1 copy.47
  178.2 1.0 fusion.19
  179.2 11.7 %cholesky.50 = f32[128,128]{1,0:T(8,128)S(1)} custom-call(f32[128,128]{1,0:T(8,128)S(1)} %cholesky.118), custom_call_target="Cholesky" | custom-call | tf_op jit(solution)/shard_map/jit(cholesky)/cholesky | solution.py:104
  190.9 0.6 compare_reduce_fusion.1
  191.5 9.8 %custom-call.18 = f32[1,128,128]{1,2,0:T(8,128)S(1)} custom-call(f32[1,128,128]{2,1,0:T(8,128)S(1)} %get-tuple-element.44), custom_call_target="InvertDiagBlocksLowerTriangular" | custom-call | tf_op jit(solution)/shard_map/jit(cholesky)/cholesky | solution.py:104
  201.4 0.2 constant_dynamic-update-slice_fusion.1
  201.6 0.3 convolution_subtract_fusion
  201.8 11.7 %cholesky.105 = f32[128,128]{1,0:T(8,128)S(1)} custom-call(f32[128,128]{1,0:T(8,128)S(1)} %convolution_subtract_fusion), custom_call_target="Cholesky" | custom-call | tf_op jit(solution)/shard_map/jit(cholesky)/cholesky | solution.py:104
  213.6 0.7 compare_reduce_fusion
  215.6 3.8 %while.1 = (s32[]{:T(128)}, f32[256,256]{1,0:T(8,128)S(1)}, s32[2,2]{1,0:T(2,128)S(1)}, f32[2,128,128]{2,1,0:T(8,128)S(1)}, s32[]{:T(128)}) while((s32[]{:T(128)}, f32[256,256]{1,0:T(8,128)S(1)}, s32[2,2]{1,0:T(2,128)S(1)}, f32[2,128,128]{2,1,0:T(8,128)S(1)}, s32[]{:T(128)}) %tuple.44), condition=%wide.while_cond, body=%wide.while_body.sunk | while | flops 2 | bytes 131189 | solution.py:105
  215.6 0.6 fusion.57
  216.2 1.3 bitcast_dynamic-update-slice_fusion.2
  217.6 0.6 fusion.57
  218.2 1.3 bitcast_dynamic-update-slice_fusion.2
  219.5 19.9 %custom-call.19 = f32[2,128,128]{1,2,0:T(8,128)S(1)} custom-call(f32[2,128,128]{2,1,0:T(8,128)S(1)} %get-tuple-element.9), custom_call_target="InvertDiagBlocksLowerTriangular" | custom-call | tf_op jit(solution)/shard_map/jit(_cho_solve)/triangular_solve | solution.py:105
  239.4 0.2 fusion.25
  239.6 0.2 fusion.5
  239.7 0.2 convolution_bitcast_fusion.3
  239.9 0.2 convolution_bitcast_fusion.2
  240.1 0.2 fusion.3
  240.3 0.2 convolution_bitcast_fusion
  240.7 13.6 %fusion.31 = f32[8,4,24,256]{3,0,2,1:T(8,128)S(1)} fusion(f32[8,4,24,256]{0,3,2,1:T(8,128)} %copy.40, f32[32,8]{1,0:T(8,128)S(1)} %reshape.171, s32[]{:T(128)S(6)} %select_n.71), kind=kOutput, calls=%fused_computation.98 | convolution fusion | flops 18874368 | bytes 1576964 | tf_op jit(solution)/shard_map/mk,mlij->klij/dot_general | solution.py:108
  254.3 0.2 reshape.172
  254.5 0.6 multiply_reduce_fusion
  255.2 0.8 fusion.20
  256.0 0.7 bitcast_multiply_fusion.1
  256.7 41.0 %all-reduce.10.cloned.1.call-done = f32[4,24,256]{2,1,0:T(8,128)} async-done(((f32[4,24,256]{2,1,0:T(8,128)}), f32[4,24,256]{2,1,0:T(8,128)}) %all-reduce.10.cloned.1.call-update) | async-done | bytes 98320 | tf_op jit(solution)/shard_map/psum | solution.py:118
  297.7 1.5 fusion.38
  (54 shorter events, 0.9 us)
Async XLA Ops:
  7.2 109.8 %all-gather.3.cloned.1.call-start = ((), (), s32[]{:S(2)}) async-start(), calls=%async_computation | async-start | bytes 2621440 | tf_op jit(solution)/shard_map/all_gather | solution.py:99
  9.0 16.9 %copy-start.5 = (f32[4,24,256]{2,1,0:T(8,128)S(1)}, f32[4,24,256]{2,1,0:T(8,128)}, u32[]{:S(2)}) copy-start(f32[4,24,256]{2,1,0:T(8,128)} %param.13) | copy-start | bytes 294916
  9.0 28.7 %collective-permute-start = (f32[40,2,256]{2,1,0:T(2,128)}, f32[40,2,256]{2,1,0:T(2,128)S(1)}, u32[]{:S(2)}, u32[]{:S(2)}) collective-permute-start(f32[40,2,256]{2,1,0:T(2,128)} %get-tuple-element.35), channel_id=1, source_target_pairs={{0,4},{4,8},{8,12},{12,16},{16,20},{20,24},{24,28},{28,0},{1,5},{5... | collective-permute-start | bytes 245768 | tf_op jit(solution)/shard_map/ppermute | solution.py:26
  9.5 28.2 %collective-permute-start.1 = (f32[40,2,256]{2,1,0:T(2,128)}, f32[40,2,256]{2,1,0:T(2,128)}, u32[]{:S(2)}, u32[]{:S(2)}) collective-permute-start(f32[40,2,256]{2,1,0:T(2,128)} %get-tuple-element.36), channel_id=1, source_target_pairs={{4,0},{8,4},{12,8},{16,12},{20,16},{24,20},{28,24},{0,28},{5,1},{9... | collective-permute-start | bytes 245768 | tf_op jit(solution)/shard_map/ppermute | solution.py:29
  28.1 9.6 %copy-start.1 = (f32[8,4,24,256]{3,2,1,0:T(8,128)S(1)}, f32[8,4,24,256]{3,2,1,0:T(8,128)}, u32[]{:S(2)}) copy-start(f32[8,4,24,256]{3,2,1,0:T(8,128)} %param.9) | copy-start | bytes 2359300
  28.1 9.6 %copy-start.3 = (f32[4,24,256]{2,1,0:T(8,128)S(1)}, f32[4,24,256]{2,1,0:T(8,128)}, u32[]{:S(2)}) copy-start(f32[4,24,256]{2,1,0:T(8,128)} %param.11) | copy-start | bytes 294916
  28.1 9.6 %copy-start.4 = (f32[4,24,256]{2,1,0:T(8,128)S(1)}, f32[4,24,256]{2,1,0:T(8,128)}, u32[]{:S(2)}) copy-start(f32[4,24,256]{2,1,0:T(8,128)} %param.10) | copy-start | bytes 294916
  40.9 0.9 copy-start.6
  42.3 17.3 %copy-start.2 = (f32[8,4,24,256]{3,2,1,0:T(8,128)}, f32[8,4,24,256]{3,2,1,0:T(8,128)S(1)}, u32[]{:S(2)}) copy-start(f32[8,4,24,256]{3,2,1,0:T(8,128)S(1)} %get-tuple-element.22) | copy-start | bytes 2359300
  53.0 6.6 %copy-start.8 = (s32[2048]{0:T(1024)S(1)}, s32[2048]{0:T(1024)}, u32[]{:S(2)}) copy-start(s32[2048]{0:T(1024)} %get-tuple-element.45) | copy-start | bytes 24580
  59.6 21.9 %copy-start.7 = (s32[2048]{0:T(1024)S(1)}, s32[2048]{0:T(1024)}, u32[]{:S(2)}) copy-start(s32[2048]{0:T(1024)} %param.14) | copy-start | bytes 24580
  59.6 21.9 %copy-start.9 = (f32[2048]{0:T(1024)S(1)}, f32[2048]{0:T(1024)}, u32[]{:S(2)}) copy-start(f32[2048]{0:T(1024)} %param.16) | copy-start | bytes 24580
  59.6 21.9 %copy-start.10 = (f32[2048]{0:T(1024)S(1)}, f32[2048]{0:T(1024)}, u32[]{:S(2)}) copy-start(f32[2048]{0:T(1024)} %param.17) | copy-start | bytes 24580
  81.5 1.6 copy-start.11
  83.0 94.0 %all-reduce.8.cloned.1.call-start = ((), (), s32[]{:S(2)}) async-start(), calls=%async_computation.1 | async-start | bytes 524288 | tf_op jit(solution)/shard_map/psum | solution.py:102
  116.9 5.1 %copy-start = (f32[256,2048]{1,0:T(8,128)S(1)}, f32[256,2048]{1,0:T(8,128)}, u32[]{:S(2)}) copy-start(f32[256,2048]{1,0:T(8,128)} %all-gather.3.cloned.1.call-done) | copy-start | bytes 6291460
  121.9 175.8 %all-reduce.10.cloned.1.call-start = ((), (), s32[]{:S(2)}) async-start(), calls=%async_computation.2 | async-start | bytes 196608 | tf_op jit(solution)/shard_map/psum | solution.py:118
Sparse Core Ops, SparseCore 0:
  83.2 33.7 all-gather.2
  122.1 54.9 all-reduce.7
  256.8 40.8 all-reduce.9
